TPU v7x, 128 devices: a whole 4x4x4 slice. The times are simulated.
128 devices in a mesh: row: 16 (over y_lo, x, core), col: 8 (over y_hi, z).
Axes of the slice: x: 4, y: 4 (y_hi: 2, y_lo: 2; y = y_hi * 2 + y_lo), z: 4, core: 2. Of those that a mesh axis runs over, the one named last changes fastest.
Arguments:
- density: bfloat16 [6144, 6144], P(('row', 'col')), may hold values from -0.49023438 to 0.49023438
- pattern: int32 [48, 48], replicated, may hold values 0 or 1
- filter_square: int32 [48, 48], replicated, may hold values 0 or 1
- filter_cube: int32 [48, 48], replicated, may hold values 0 or 1
Outputs:
- purified: float32 [6144, 6144], P('row', 'col')
All inputs are finite; a program needn't handle non-finite values.
Results may differ from a plain program's by a relative error of at most 0.0027.
Values may be sent and summed in bfloat16 or wider, within the bound.
A program may use at most 64 MiB of HBM per device.

v0:
```python
import jax
import jax.numpy as jnp
from jax import lax
from jax.sharding import PartitionSpec as P

BLK = 128


def tile_mask(mask, row_id, col_id, rows, width):
    row_blocks = rows // BLK
    col_blocks = width // BLK
    small = lax.dynamic_slice(
        mask, (row_id * row_blocks, col_id * col_blocks), (row_blocks, col_blocks)
    ).astype(jnp.float32)
    return jnp.broadcast_to(small[:, None, :, None], (row_blocks, BLK, col_blocks, BLK)).reshape(
        rows, width
    )


def on_device(density, pattern, filter_square, filter_cube):
    row_count = lax.axis_size("row")
    col_count = lax.axis_size("col")
    row_id = lax.axis_index("row")
    col_id = lax.axis_index("col")
    rows_one, order = density.shape
    nblocks = pattern.shape[0]
    rows = order // row_count
    width = order // col_count
    first = (row_id * col_count + col_id) * rows_one
    block_of = (first + jnp.arange(rows_one, dtype=jnp.int32)) // BLK
    row_mask = jnp.take(pattern, block_of, axis=0).astype(jnp.bfloat16)
    full_mask = jnp.broadcast_to(row_mask[:, :, None], (rows_one, nblocks, BLK)).reshape(
        rows_one, order
    )
    local = density * full_mask
    left = lax.all_gather(local, "col", axis=0, tiled=True)
    tile = lax.dynamic_slice(left, (0, col_id * width), (rows, width))
    right = lax.all_gather(tile, "row", axis=0, tiled=True)
    square = jnp.dot(left, right, preferred_element_type=jnp.float32)
    square = square * tile_mask(filter_square, row_id, col_id, rows, width)
    half = lax.all_gather(square.astype(jnp.bfloat16), "row", axis=0, tiled=True)
    cube = jnp.dot(left, half, preferred_element_type=jnp.float32)
    cube = cube * tile_mask(filter_cube, row_id, col_id, rows, width)
    return 3.0 * square - 2.0 * cube


def solution(mesh):
    placed = (P(("row", "col"), None), P(), P(), P())
    return jax.shard_map(
        on_device, mesh=mesh, in_specs=placed, out_specs=P("row", "col"), check_vma=False
    )
```

profile of v0, /device:TPU:1, one launch (start us, length us, event | category | flops | bytes accessed | tf_op | source)
XLA Modules:
  0.0 231.8 jit_solution(9919951318664396545)
XLA Ops:
  6.5 0.0 copy-start
  6.5 0.0 all-gather.4.cloned.1.call-start
  6.6 0.7 copy-done
  7.3 0.6 gather_fusion
  7.9 0.1 select_convert_fusion
  7.9 0.4 broadcast_in_dim.30
  8.3 2.0 bitcast_multiply_fusion
  10.3 0.0 all-gather.4.cloned.1.call-update
  10.4 0.0 all-gather.6.cloned.1.call-start
  10.4 78.9 %all-gather.4.cloned.1.call-done = bf16[384,6144]{1,0:T(8,128)(2,1)} async-done(((bf16[48,6144]{1,0:T(8,128)(2,1)}), bf16[384,6144]{1,0:T(8,128)(2,1)}) %all-gather.4.cloned.1.call-update) | async-done | bytes 4718608 | tf_op jit(solution)/shard_map/all_gather | solution.py:36
  89.3 1.9 constant_dynamic-slice_fusion
  91.2 0.0 all-gather.6.cloned.1.call-update
  91.2 0.0 all-gather.8.cloned.1.call-start
  91.3 0.8 dynamic-slice_convert_fusion
  92.1 54.9 %all-gather.6.cloned.1.call-done = bf16[6144,768]{1,0:T(8,128)(2,1)} async-done(((bf16[384,768]{1,0:T(8,128)(2,1)}), bf16[6144,768]{1,0:T(8,128)(2,1)}) %all-gather.6.cloned.1.call-update) | async-done | bytes 9437200 | tf_op jit(solution)/shard_map/all_gather | solution.py:38
  146.9 0.2 broadcast_in_dim.31
  147.1 9.8 %fusion.3 = (bf16[384,768]{1,0:T(8,128)(2,1)}, f32[384,768]{1,0:T(8,128)S(1)}) fusion(f32[48,8,6,128]{3,2,1,0:T(8,128)S(1)} %bitcast.18, bf16[384,6144]{1,0:T(8,128)(2,1)} %all-gather.4.cloned.1.call-done, bf16[6144,768]{1,0:T(8,128)(2,1)} %all-gather.6.cloned.1.call-done), kind=kOutput, calls=%fused_computation.23 | convolution fusion | flops 3624468480 | bytes 17104896 | tf_op jit(solution)/shard_map/dot_general | solution.py:39
  156.9 0.0 all-gather.8.cloned.1.call-update
  156.9 58.1 %all-gather.8.cloned.1.call-done = bf16[6144,768]{1,0:T(8,128)(2,1)} async-done(((bf16[384,768]{1,0:T(8,128)(2,1)}), bf16[6144,768]{1,0:T(8,128)(2,1)}) %all-gather.8.cloned.1.call-update) | async-done | bytes 9437200 | tf_op jit(solution)/shard_map/all_gather | solution.py:41
  215.0 0.2 broadcast_in_dim.32
  215.1 10.1 %fusion.1 = f32[384,768]{1,0:T(8,128)} fusion(bf16[384,6144]{1,0:T(8,128)(2,1)} %all-gather.4.cloned.1.call-done, bf16[6144,768]{1,0:T(8,128)(2,1)} %all-gather.8.cloned.1.call-done, f32[48,8,6,128]{3,2,1,0:T(8,128)S(1)} %bitcast.19, f32[384,768]{1,0:T(8,128)S(1)} %get-tuple-element.6), kind=kOutput, calls=%fused_computation.4 | convolution fusion | flops 3625058304 | bytes 17694720 | tf_op jit(solution)/shard_map/dot_general | solution.py:42
  (3 shorter events, 0.0 us)
Async XLA Ops:
  6.5 0.7 copy-start
  6.5 82.7 %all-gather.4.cloned.1.call-start = ((), (), s32[]{:S(2)}) async-start(), calls=%async_computation | async-start | bytes 5308416 | tf_op jit(solution)/shard_map/all_gather | solution.py:36
  10.4 136.6 %all-gather.6.cloned.1.call-start = ((), (), s32[]{:S(2)}) async-start(), calls=%async_computation.1 | async-start | bytes 10027008 | tf_op jit(solution)/shard_map/all_gather | solution.py:38
  91.2 123.7 %all-gather.8.cloned.1.call-start = ((), (), s32[]{:S(2)}) async-start(), calls=%async_computation.2 | async-start | bytes 10027008 | tf_op jit(solution)/shard_map/all_gather | solution.py:41
Sparse Core Ops, SparseCore 0:
  10.5 78.7 all-gather.3
  91.3 55.5 all-gather.5
  157.0 57.8 all-gather.7
where the time goes:
time: 232 us
  waiting for transfers between devices  192 us (83%)
  matrix products  19.9 us (9%)
  between operations  13.2 us (6%)
  local copies, waits for them, and re-layouts  3.89 us (2%)
  other arithmetic  2.93 us (1%)
    all_gather x1, waiting for transfers between devices, on_device(): left = lax.all_gather(local, 'col', axis=0, tiled=True)  78.9 us
    all_gather x1, waiting for transfers between devices, on_device(): lax.all_gather(square.astype(jnp.bfloat16), 'row', axis=0, tiled=True)  58.1 us
    all_gather x1, waiting for transfers between devices, on_device(): right = lax.all_gather(tile, 'row', axis=0, tiled=True)  54.9 us
    dot_general x1, matrix products, on_device(): cube = jnp.dot(left, half, preferred_element_type=jnp.float32)  10.1 us
    dot_general x1, matrix products, on_device(): square = jnp.dot(left, right, preferred_element_type=jnp.float32)  9.77 us
  transfers between devices with their start and end apart: 3, of which 3 were waited for; matrix products, arithmetic and copies ran while one was open for 0% of the time, Pallas kernels for 0%

commit v1 on v0

--- a/solution.py
+++ b/solution.py
@@ -2,6 +2,7 @@
 import jax.numpy as jnp
 from jax import lax
 from jax.sharding import PartitionSpec as P
+from jax.lax import all_to_all, axis_size
 
 BLK = 128
 
@@ -33,7 +34,9 @@
         rows_one, order
     )
     local = density * full_mask
-    left = lax.all_gather(local, "col", axis=0, tiled=True)
+    left = jnp.concatenate(
+        all_to_all(jnp.stack([local for _ in range(axis_size("col"))]), "col", 0, 0), axis=0
+    )
     tile = lax.dynamic_slice(left, (0, col_id * width), (rows, width))
     right = lax.all_gather(tile, "row", axis=0, tiled=True)
     square = jnp.dot(left, right, preferred_element_type=jnp.float32)

time: 232 us -> 220 us (0.948)
  waiting for transfers between devices: 192 us -> 169 us
  starting transfers between devices: 0.09 us -> 8.57 us
  local copies, waits for them, and re-layouts: 3.89 us -> 6.6 us
    all_gather x1 -> x0, waiting for transfers between devices: 78.9 us -> none  [on_device(): left = lax.all_gather(local, 'col', axis=0, tiled=True)]
    all_to_all x0 -> x1, waiting for transfers between devices: none -> 54.3 us  [on_device(): all_to_all(jnp.stack([local for _ in range(axis_size('col'))]), 'col', 0, 0)]
    all_to_all x0 -> x1, starting transfers between devices: none -> 8.49 us  [on_device(): all_to_all(jnp.stack([local for _ in range(axis_size('col'))]), 'col', 0, 0)]
    another operation x0 -> x1, local copies, waits for them, and re-layouts: none -> 2.7 us  [on_device(): jnp.stack([local for _ in range(axis_size('col'))])]
where the time goes in v1:
time: 220 us; the launch traced here: 219 us
  waiting for transfers between devices  169 us (77%)
  matrix products  19.9 us (9%)
  between operations  13.5 us (6%)
  starting transfers between devices  8.57 us (4%)
  local copies, waits for them, and re-layouts  6.6 us (3%)
    all_gather x1, waiting for transfers between devices, on_device(): lax.all_gather(square.astype(jnp.bfloat16), 'row', axis=0, tiled=True)  58.1 us
    all_gather x1, waiting for transfers between devices, on_device(): right = lax.all_gather(tile, 'row', axis=0, tiled=True)  56.5 us
    all_to_all x1, waiting for transfers between devices, on_device(): all_to_all(jnp.stack([local for _ in range(axis_size('col'))]), 'col', 0, 0)  54.3 us
    dot_general x1, matrix products, on_device(): cube = jnp.dot(left, half, preferred_element_type=jnp.float32)  10.1 us
    dot_general x1, matrix products, on_device(): square = jnp.dot(left, right, preferred_element_type=jnp.float32)  9.77 us
    all_to_all x1, starting transfers between devices, on_device(): all_to_all(jnp.stack([local for _ in range(axis_size('col'))]), 'col', 0, 0)  8.49 us
  transfers between devices with their start and end apart: 3, of which 3 were waited for; matrix products, arithmetic and copies ran while one was open for 0% of the time, Pallas kernels for 0%

profile of v1, /device:TPU:1, one launch (start us, length us, event | category | flops | bytes accessed | tf_op | source)
XLA Modules:
  0.0 219.5 jit_solution(2784126029004024277)
XLA Ops:
  6.5 0.0 copy-start
  6.6 0.7 copy-done
  7.3 0.6 gather_fusion
  7.9 0.1 select_convert_fusion
  7.9 0.4 broadcast_in_dim.30
  8.3 1.2 bitcast_multiply_fusion
  9.5 2.7 %stack.2 = bf16[8,48,6144]{2,1,0:T(8,128)(2,1)} broadcast(bf16[48,6144]{1,0:T(8,128)(2,1)S(1)} %bitcast_multiply_fusion), dimensions={1,2} | broadcast | bytes 5308416 | tf_op jit(solution)/shard_map/stack | solution.py:38
  12.2 8.5 %all-to-all-start = ((bf16[8,48,6144]{2,1,0:T(8,128)(2,1)}), bf16[8,48,6144]{2,1,0:T(8,128)(2,1)}, u32[]{:S(2)}, u32[]{:S(2)}) async-start(bf16[8,48,6144]{2,1,0:T(8,128)(2,1)} %stack.2), calls=%async_computation | async-start | bytes 9437184 | tf_op jit(solution)/shard_map/all_to_all | solution.py:38
  20.7 0.0 all-gather.3.cloned.1.call-start
  20.8 54.3 %all-to-all-done = bf16[8,48,6144]{2,1,0:T(8,128)(2,1)} async-done(((bf16[8,48,6144]{2,1,0:T(8,128)(2,1)}), bf16[8,48,6144]{2,1,0:T(8,128)(2,1)}, u32[]{:S(2)}, u32[]{:S(2)}) %all-to-all-start) | async-done | bytes 4718624 | tf_op jit(solution)/shard_map/all_to_all | solution.py:38
  75.1 1.9 constant_dynamic-slice_fusion
  77.0 0.0 all-gather.3.cloned.1.call-update
  77.0 0.0 all-gather.5.cloned.1.call-start
  77.0 0.8 dynamic-slice_convert_fusion
  77.8 56.5 %all-gather.3.cloned.1.call-done = bf16[6144,768]{1,0:T(8,128)(2,1)} async-done(((bf16[384,768]{1,0:T(8,128)(2,1)}), bf16[6144,768]{1,0:T(8,128)(2,1)}) %all-gather.3.cloned.1.call-update) | async-done | bytes 9437200 | tf_op jit(solution)/shard_map/all_gather | solution.py:41
  134.3 0.2 broadcast_in_dim.31
  134.5 9.8 %fusion.3 = (bf16[384,768]{1,0:T(8,128)(2,1)}, f32[384,768]{1,0:T(8,128)S(1)}) fusion(f32[48,8,6,128]{3,2,1,0:T(8,128)S(1)} %bitcast.19, bf16[384,6144]{1,0:T(8,128)(2,1)} %bitcast.1, bf16[6144,768]{1,0:T(8,128)(2,1)} %all-gather.3.cloned.1.call-done), kind=kOutput, calls=%fused_computation.23 | convolution fusion | flops 3624468480 | bytes 17104896 | tf_op jit(solution)/shard_map/dot_general | solution.py:42
  144.3 0.0 all-gather.5.cloned.1.call-update
  144.3 58.1 %all-gather.5.cloned.1.call-done = bf16[6144,768]{1,0:T(8,128)(2,1)} async-done(((bf16[384,768]{1,0:T(8,128)(2,1)}), bf16[6144,768]{1,0:T(8,128)(2,1)}) %all-gather.5.cloned.1.call-update) | async-done | bytes 9437200 | tf_op jit(solution)/shard_map/all_gather | solution.py:44
  202.4 0.2 broadcast_in_dim.32
  202.5 10.1 %fusion.1 = f32[384,768]{1,0:T(8,128)} fusion(bf16[384,6144]{1,0:T(8,128)(2,1)} %bitcast.1, bf16[6144,768]{1,0:T(8,128)(2,1)} %all-gather.5.cloned.1.call-done, f32[48,8,6,128]{3,2,1,0:T(8,128)S(1)} %bitcast.20, f32[384,768]{1,0:T(8,128)S(1)} %get-tuple-element.6), kind=kOutput, calls=%fused_computation.4 | convolution fusion | flops 3625058304 | bytes 17694720 | tf_op jit(solution)/shard_map/dot_general | solution.py:45
  (3 shorter events, 0.0 us)
Async XLA Ops:
  6.5 0.7 copy-start
  12.2 62.8 %all-to-all-start = ((bf16[8,48,6144]{2,1,0:T(8,128)(2,1)}), bf16[8,48,6144]{2,1,0:T(8,128)(2,1)}, u32[]{:S(2)}, u32[]{:S(2)}) async-start(bf16[8,48,6144]{2,1,0:T(8,128)(2,1)} %stack.2), calls=%async_computation | async-start | bytes 9437184 | tf_op jit(solution)/shard_map/all_to_all | solution.py:38
  20.7 113.6 %all-gather.3.cloned.1.call-start = ((), (), s32[]{:S(2)}) async-start(), calls=%async_computation.1 | async-start | bytes 10027008 | tf_op jit(solution)/shard_map/all_gather | solution.py:41
  77.0 125.4 %all-gather.5.cloned.1.call-start = ((), (), s32[]{:S(2)}) async-start(), calls=%async_computation.2 | async-start | bytes 10027008 | tf_op jit(solution)/shard_map/all_gather | solution.py:44
Sparse Core Ops, SparseCore 0:
  77.1 57.1 all-gather.2
  144.4 57.8 all-gather.4
